TPU v7x, 32 devices: a whole 2x2x4 slice. The times are simulated.
32 devices in a mesh: wide: 8 (over y, x, core), blk: 4 (over z).
Axes of the slice: x: 2, y: 2, z: 4, core: 2. Of those that a mesh axis runs over, the one named last changes fastest.
Arguments:
- left_points: float32 [4096], P(('wide', 'blk')), may hold values from -1 to 1, as said below
- left_ports: int32 [4096], P(('wide', 'blk')), may hold values from 0 to 63
- left_values: bfloat16 [4096, 64], P(('wide', 'blk')), may hold values from -6 to 6
- right_points: float32 [2048], P('blk'), may hold values from -1 to 1
- right_ports: int32 [2048], P('blk'), may hold values from 0 to 63
- right_values: bfloat16 [2048, 64], P('blk'), may hold values from -6 to 6
- sketch_block: int32 [2048], P('blk'), may hold values from 0 to 63, as said below
- sketch_weight: bfloat16 [2048], P('blk'), may hold values from -1 to 1
Outputs:
- basis: float32 [4096, 64], P(('wide', 'blk'))
- projected: float32 [64, 64], replicated
Inputs may be any that keep to these rules, and one draw needn't show every extreme that they name: `left_points`: no left point lies closer than 0.6 / 2048 to any right point. `sketch_block`: in every aligned run of 64 right samples each sketch column appears exactly once.
All inputs are finite; a program needn't handle non-finite values.
Results may differ from a plain program's by a relative error of at most 0.0019.
Values sent between devices are 32-bit elements; how exact they have to be, the bound alone decides.
No kernel may reach another device: no remote copies, remote signals or barrier semaphores. Data moves between devices by JAX's collectives and lax.ppermute only.
A program may use at most 64 MiB of HBM per device.

v0:
```python
import jax
import jax.numpy as jnp
from jax import lax
from jax.sharding import PartitionSpec as P

K = 64


def cholesky_lower(gram):
    order = gram.shape[0]
    index_ids = jnp.arange(order, dtype=jnp.int32)

    def column_step(j, lower):
        row_j = lax.dynamic_slice_in_dim(lower, j, 1, 0)[0]
        column = lax.dynamic_slice_in_dim(gram, j, 1, 1)[:, 0] - jnp.dot(
            lower, row_j, precision=lax.Precision.HIGHEST
        )
        pivot = jnp.sqrt(lax.dynamic_slice_in_dim(column, j, 1, 0)[0])
        fresh = jnp.where(
            index_ids > j,
            column / pivot,
            jnp.where(index_ids == j, pivot, jnp.zeros((), gram.dtype)),
        )
        marker = (index_ids == j).astype(gram.dtype)
        return lower + fresh[:, None] * marker[None, :]

    return lax.fori_loop(0, order, column_step, jnp.zeros_like(gram))


def solve_lower(lower, rhs):
    order = lower.shape[0]
    index_ids = jnp.arange(order, dtype=jnp.int32)

    def row_step(j, result):
        row_j = lax.dynamic_slice_in_dim(lower, j, 1, 0)[0]
        pivot = lax.dynamic_slice_in_dim(row_j, j, 1, 0)[0]
        target = lax.dynamic_slice_in_dim(rhs, j, 1, 0)[0]
        value = (target - jnp.dot(row_j, result, precision=lax.Precision.HIGHEST)) / pivot
        marker = (index_ids == j).astype(rhs.dtype)
        return result + marker[:, None] * value[None, :]

    return lax.fori_loop(0, order, row_step, jnp.zeros_like(rhs))


def solve_upper(upper, rhs):
    order = upper.shape[0]
    index_ids = jnp.arange(order, dtype=jnp.int32)

    def row_step(step, result):
        j = order - 1 - step
        row_j = lax.dynamic_slice_in_dim(upper, j, 1, 0)[0]
        pivot = lax.dynamic_slice_in_dim(row_j, j, 1, 0)[0]
        target = lax.dynamic_slice_in_dim(rhs, j, 1, 0)[0]
        value = (target - jnp.dot(row_j, result, precision=lax.Precision.HIGHEST)) / pivot
        marker = (index_ids == j).astype(rhs.dtype)
        return result + marker[:, None] * value[None, :]

    return lax.fori_loop(0, order, row_step, jnp.zeros_like(rhs))


def tile_sketch(left_freq, left_onehot, left_values, points, ports, values_block, columns, weights):
    amount = points.shape[0]
    block_count = amount // amount
    port_ids = jnp.arange(left_values.shape[1], dtype=jnp.int32)
    column_ids = jnp.arange(K, dtype=jnp.int32)

    def absorb(carry, items):
        freq, port_block, value_rows, column_block, weight_block = items
        onehot_right = (port_ids[:, None] == port_block[None, :]).astype(jnp.float32)
        num_v = jnp.dot(
            left_values,
            onehot_right,
            precision=lax.Precision.HIGHEST,
            preferred_element_type=jnp.float32,
        )
        num_w = lax.dot_general(
            left_onehot,
            value_rows,
            (((1,), (1,)), ((), ())),
            precision=lax.Precision.HIGHEST,
            preferred_element_type=jnp.float32,
        )
        inverse = 1.0 / (left_freq[:, None] - freq[None, :])
        loewner = (num_v - num_w) * inverse
        shifted = (left_freq[:, None] * num_v - freq[None, :] * num_w) * inverse
        omega = jnp.where(
            column_block[:, None] == column_ids[None, :],
            weight_block[:, None],
            jnp.zeros((), jnp.float32),
        )
        sketch_part = jnp.dot(
            loewner, omega, precision=lax.Precision.HIGHEST, preferred_element_type=jnp.float32
        )
        shift_part = jnp.dot(
            shifted, omega, precision=lax.Precision.HIGHEST, preferred_element_type=jnp.float32
        )
        return ((carry[0] + sketch_part, carry[1] + shift_part), None)

    row_count = left_values.shape[0]
    start_carry = (jnp.zeros((row_count, K), jnp.float32), jnp.zeros((row_count, K), jnp.float32))
    items = (
        points.reshape(block_count, amount),
        ports.reshape(block_count, amount),
        values_block.reshape(block_count, amount, values_block.shape[1]),
        columns.reshape(block_count, amount),
        weights.reshape(block_count, amount),
    )
    result, _ = lax.scan(absorb, start_carry, items)
    return result


def left_setup(points, ports, width):
    port_ids = jnp.arange(width, dtype=jnp.int32)
    onehot_left = (ports[:, None] == port_ids[None, :]).astype(jnp.float32)
    return (points, onehot_left)


def per_device(
    left_points,
    left_ports,
    left_values,
    right_points,
    right_ports,
    right_values,
    sketch_block,
    sketch_weight,
):
    row_count = left_points.shape[0]
    width = left_values.shape[1]
    left_wide = left_values.astype(jnp.float32)
    group_points, group_ports, group_values = (
        lax.all_gather(left_points, "blk", axis=0, tiled=True),
        lax.all_gather(left_ports, "blk", axis=0, tiled=True),
        lax.all_gather(left_wide, "blk", axis=0, tiled=True),
    )
    right_wide = right_values.astype(jnp.float32)
    weight_wide = sketch_weight.astype(jnp.float32)
    left_freq, left_onehot = left_setup(group_points, group_ports, width)
    sketch_part, shift_part = tile_sketch(
        left_freq,
        left_onehot,
        group_values,
        right_points,
        right_ports,
        right_wide,
        sketch_block,
        weight_wide,
    )
    stacked = lax.psum_scatter(
        jnp.concatenate([sketch_part, shift_part], axis=1), "blk", scatter_dimension=0, tiled=True
    )
    sketch = stacked[:, :K]
    shifted_sketch = stacked[:, K:]
    row_total = row_count * lax.axis_size("wide") * lax.axis_size("blk")
    gram_local = jnp.dot(sketch.T, sketch, precision=lax.Precision.HIGHEST)
    gram = lax.psum(gram_local, ("wide", "blk")) / row_total
    lower = cholesky_lower(gram)
    basis_t = solve_lower(lower, sketch.T)
    projection_local = jnp.dot(basis_t, shifted_sketch, precision=lax.Precision.HIGHEST)
    coefficient = lax.psum(projection_local, ("wide", "blk")) / row_total
    projected = solve_upper(lower.T, coefficient)
    return (basis_t.T, projected)


def solution(mesh):
    placed = (
        P(("wide", "blk")),
        P(("wide", "blk")),
        P(("wide", "blk"), None),
        P("blk"),
        P("blk"),
        P("blk", None),
        P("blk"),
        P("blk"),
    )
    return jax.shard_map(
        per_device,
        mesh=mesh,
        in_specs=placed,
        out_specs=(P(("wide", "blk"), None), P()),
        check_vma=False,
    )
```

profile of v0, /device:TPU:0, one launch (start us, length us, event | category | flops | bytes accessed | tf_op | source)
XLA Modules:
  0.0 438.6 jit_solution(5190188491721261414)
XLA Ops:
  7.9 15.1 %all_gather.9 = f32[512,64]{0,1:T(8,128)S(1)} all-gather(f32[128,64]{0,1:T(8,128)S(1)} %convert_element_type.55), channel_id=1, replica_groups=mesh['wide'=8,'blk'=4] {'blk'}, dimensions={0}, use_global_device_ids=true | all-gather | bytes 163840 | tf_op jit(solution)/shard_map/all_gather | solution.py:134
  23.7 11.2 %all-gather = s32[4,1,128]{2,1,0:T(1,128)S(1)} all-gather(s32[1,1,128]{2,1,0:T(1,128)S(1)} %bitcast.82), channel_id=1, replica_groups=mesh['wide'=8,'blk'=4] {'blk'}, dimensions={0}, use_global_device_ids=true | all-gather | bytes 2560 | tf_op jit(solution)/shard_map/all_gather | solution.py:133
  35.6 7.7 %all-gather.1 = f32[4,1,128]{2,1,0:T(1,128)S(1)} all-gather(f32[1,1,128]{2,1,0:T(1,128)S(1)} %bitcast.83), channel_id=1, replica_groups=mesh['wide'=8,'blk'=4] {'blk'}, dimensions={0}, use_global_device_ids=true | all-gather | bytes 2560 | tf_op jit(solution)/shard_map/all_gather | solution.py:132
  45.3 1.1 fusion.28
  46.4 1.0 fusion.33
  48.1 19.8 %reduce-scatter.2.cloned.1.call-done = f32[128,128]{0,1:T(8,128)} async-done(((f32[512,128]{0,1:T(8,128)}), f32[128,128]{0,1:T(8,128)}) %reduce-scatter.2.cloned.1.call-update) | async-done | bytes 65552 | tf_op jit(solution)/shard_map/reduce_scatter | solution.py:149
  67.9 1.0 fusion.55
  68.9 38.6 %psum.14 = f32[64,64]{1,0:T(8,128)S(1)} all-reduce(f32[64,64]{1,0:T(8,128)S(1)} %fusion.55), channel_id=1, replica_groups=mesh['wide'=8,'blk'=4] {'wide','blk'}, use_global_device_ids=true, to_apply=%region_1.2 | all-reduce | flops 4096 | bytes 32768 | tf_op jit(solution)/shard_map/psum | solution.py:156
  107.7 94.5 %while.57 = (s32[]{:T(128)}, f32[64,64]{1,0:T(8,128)S(1)}, f32[64,64]{0,1:T(8,128)S(1)}, s32[]{:T(128)}, s32[]{:T(128)}) while((s32[]{:T(128)}, f32[64,64]{1,0:T(8,128)S(1)}, f32[64,64]{0,1:T(8,128)S(1)}, s32[]{:T(128)}, s32[]{:T(128)}) %tuple.124), condition=%wide.region_3.4_spmd.clone.clone, body=%wide.region_2.3_spmd.clone.clone.sunk | while | flops 66051 | bytes 101992 | solution.py:27
  202.2 93.7 %while.55 = (s32[]{:T(128)}, f32[64,128]{1,0:T(8,128)S(1)}, f32[64,128]{1,0:T(8,128)S(1)}, f32[64,64]{1,0:T(8,128)S(1)}, s32[]{:T(128)}, /*index=5*/s32[]{:T(128)}, s32[]{:T(128)}) while((s32[]{:T(128)}, f32[64,128]{1,0:T(8,128)S(1)}, f32[64,128]{1,0:T(8,128)S(1)}, f32[64,64]{1,0:T(8,128)S(1)}, s32[]{:T(128)}, ...), condition=%wide.region_5.6_spmd.clone, body=%wide.region_4.5_spmd.clone.sunk | while | flops 131460 | bytes 102520 | solution.py:42
  202.8 0.8 fusion.76
  204.3 0.8 fusion.76
  205.7 0.8 fusion.76
  207.2 0.8 fusion.76
  208.7 0.8 fusion.76
  210.1 0.8 fusion.76
  211.6 0.8 fusion.76
  213.1 0.8 fusion.76
  214.5 0.8 fusion.76
  216.0 0.8 fusion.76
  217.5 0.8 fusion.76
  218.9 0.8 fusion.76
  220.4 0.8 fusion.76
  221.8 0.8 fusion.76
  223.3 0.8 fusion.76
  224.8 0.8 fusion.76
  226.2 0.8 fusion.76
  227.7 0.8 fusion.76
  229.2 0.8 fusion.76
  230.6 0.8 fusion.76
  232.1 0.8 fusion.76
  233.6 0.8 fusion.76
  235.0 0.8 fusion.76
  236.5 0.8 fusion.76
  238.0 0.8 fusion.76
  239.4 0.8 fusion.76
  240.9 0.8 fusion.76
  242.3 0.8 fusion.76
  243.8 0.8 fusion.76
  245.3 0.8 fusion.76
  246.7 0.8 fusion.76
  248.2 0.8 fusion.76
  249.7 0.8 fusion.76
  251.1 0.8 fusion.76
  254.1 0.8 fusion.76
  273.1 0.8 fusion.76
  276.0 0.8 fusion.76
  279.0 0.8 fusion.76
  281.9 0.8 fusion.76
  296.6 40.8 %psum.15 = f32[64,64]{1,0:T(8,128)S(1)} all-reduce(f32[64,64]{1,0:T(8,128)S(1)} %fusion.53), channel_id=1, replica_groups=mesh['wide'=8,'blk'=4] {'wide','blk'}, use_global_device_ids=true, to_apply=%region_6.7 | all-reduce | flops 4096 | bytes 32768 | tf_op jit(solution)/shard_map/psum | solution.py:160
  337.5 93.7 %while.56 = (s32[]{:T(128)}, f32[64,64]{1,0:T(8,128)S(1)}, f32[64,64]{1,0:T(8,128)S(1)}, f32[64,64]{1,0:T(8,128)S(1)}, s32[]{:T(128)}, /*index=5*/s32[]{:T(128)}, s32[]{:T(128)}, s32[]{:T(128)}) while((s32[]{:T(128)}, f32[64,64]{1,0:T(8,128)S(1)}, f32[64,64]{1,0:T(8,128)S(1)}, f32[64,64]{1,0:T(8,128)S(1)}, s32[]{:T(128)}, ...), condition=%wide.region_8.9_spmd.clone, body=%wide.region_7.8_spmd.clone.sunk | while | flops 65800 | bytes 69297 | solution.py:58
  342.5 0.8 fusion.79
  348.3 0.8 fusion.79
  355.6 0.8 fusion.79
  363.0 0.8 fusion.79
  370.3 0.8 fusion.79
  376.1 0.8 fusion.79
  383.5 0.8 fusion.79
  390.8 0.8 fusion.79
  398.1 0.8 fusion.79
  403.9 0.8 fusion.79
  411.3 0.8 fusion.79
  418.6 0.8 fusion.79
  425.9 0.8 fusion.79
  (880 shorter events, 207.0 us)
Async XLA Ops:
  7.2 37.4 %copy-start = (bf16[512,64]{0,1:T(8,128)(2,1)S(1)}, bf16[512,64]{0,1:T(8,128)(2,1)}, u32[]{:S(2)}) copy-start(bf16[512,64]{0,1:T(8,128)(2,1)} %param.19) | copy-start | bytes 196612
  7.2 60.7 %reduce-scatter.2.cloned.1.call-start = ((), (), s32[]{:S(2)}) async-start(), calls=%async_computation.1 | async-start | bytes 327680 | tf_op jit(solution)/shard_map/reduce_scatter | solution.py:149
  23.0 0.7 copy-start.6
  34.9 0.7 copy-start.7
  35.6 7.7 %copy-start.5 = (bf16[512]{0:T(512)(128)(2,1)S(1)}, bf16[512]{0:T(512)(128)(2,1)}, u32[]{:S(2)}) copy-start(bf16[512]{0:T(512)(128)(2,1)} %param.21) | copy-start | bytes 3076
  43.3 0.7 copy-start.4
  44.6 0.7 copy-start.8
  44.6 0.7 copy-start.9
  107.7 94.5 %copy-start.3 = (f32[128,128]{0,1:T(8,128)S(1)}, f32[128,128]{0,1:T(8,128)}, u32[]{:S(2)}) copy-start(f32[128,128]{0,1:T(8,128)} %reduce-scatter.2.cloned.1.call-done) | copy-start | bytes 196612
  295.9 0.6 copy-start.1
  431.2 0.6 copy-start.2
Sparse Core Ops, SparseCore 0:
  48.2 19.6 reduce-scatter.1
where the time goes:
time: 441 us; the launch traced here: 439 us
  local copies, waits for them, and re-layouts  119 us (27%)
  matrix products  114 us (26%)
  blocking collectives  113 us (26%)
  loops' own time  40.3 us (9%)
  waiting for transfers between devices  19.8 us (4%)
  other arithmetic  18.2 us (4%)
  between operations  14.2 us (3%)
    dot_general x128, matrix products, row_step(): jnp.dot(row_j, result, precision=lax.Precision.HIGHEST)  100 us
    dynamic_slice x128, local copies, waits for them, and re-layouts, row_step(): pivot = lax.dynamic_slice_in_dim(row_j, j, 1, 0)[0]  76.2 us
    psum x1, blocking collectives, per_device(): coefficient = lax.psum(projection_local, ('wide', 'blk')) / row_total  40.8 us
    another operation x1, loops' own time, cholesky_lower(): return lax.fori_loop(0, order, column_step, jnp.zeros_like(gram))  40 us
    dynamic_slice x64, local copies, waits for them, and re-layouts, column_step(): pivot = jnp.sqrt(lax.dynamic_slice_in_dim(column, j, 1, 0)[0])  39.2 us
    psum x1, blocking collectives, per_device(): gram = lax.psum(gram_local, ('wide', 'blk')) / row_total  38.6 us
    reduce_scatter x1, waiting for transfers between devices, per_device(): lax.psum_scatter(jnp.concatenate([sketch_part, shift_part], axis=1), 'blk...  19.8 us
    all_gather x1, blocking collectives, per_device(): lax.all_gather(left_wide, 'blk', axis=0, tiled=True)  15.1 us
  transfers between devices with their start and end apart: 1, of which 1 were waited for; matrix products, arithmetic and copies ran while one was open for 0% of the time, Pallas kernels for 0%

commit v1 on v0

--- a/solution.py
+++ b/solution.py
@@ -157,7 +157,7 @@
     lower = cholesky_lower(gram)
     basis_t = solve_lower(lower, sketch.T)
     projection_local = jnp.dot(basis_t, shifted_sketch, precision=lax.Precision.HIGHEST)
-    coefficient = lax.psum(projection_local, ("wide", "blk")) / row_total
+    coefficient = jnp.sum(lax.all_gather(projection_local, ("wide", "blk")), axis=0) / row_total
     projected = solve_upper(lower.T, coefficient)
     return (basis_t.T, projected)
 

time: 441 us -> 476 us (1.079)
  blocking collectives: 113 us -> 148 us
    all_gather x0 -> x1, blocking collectives: none -> 75.5 us  [per_device(): lax.all_gather(projection_local, ('wide', 'blk'))]
    psum x1 -> x0, blocking collectives: 40.8 us -> none  [per_device(): coefficient = lax.psum(projection_local, ('wide', 'blk')) / row_total]
where the time goes in v1:
time: 476 us; the launch traced here: 473 us
  blocking collectives  148 us (31%)
  local copies, waits for them, and re-layouts  119 us (25%)
  matrix products  114 us (24%)
  loops' own time  40.3 us (8%)
  waiting for transfers between devices  19.8 us (4%)
  other arithmetic  18.3 us (4%)
  between operations  14.2 us (3%)
    dot_general x128, matrix products, row_step(): jnp.dot(row_j, result, precision=lax.Precision.HIGHEST)  100 us
    dynamic_slice x128, local copies, waits for them, and re-layouts, row_step(): pivot = lax.dynamic_slice_in_dim(row_j, j, 1, 0)[0]  76.2 us
    all_gather x1, blocking collectives, per_device(): lax.all_gather(projection_local, ('wide', 'blk'))  75.5 us
    another operation x1, loops' own time, cholesky_lower(): return lax.fori_loop(0, order, column_step, jnp.zeros_like(gram))  40 us
    dynamic_slice x64, local copies, waits for them, and re-layouts, column_step(): pivot = jnp.sqrt(lax.dynamic_slice_in_dim(column, j, 1, 0)[0])  39.2 us
    psum x1, blocking collectives, per_device(): gram = lax.psum(gram_local, ('wide', 'blk')) / row_total  38.6 us
    reduce_scatter x1, waiting for transfers between devices, per_device(): lax.psum_scatter(jnp.concatenate([sketch_part, shift_part], axis=1), 'blk...  19.8 us
    all_gather x1, blocking collectives, per_device(): lax.all_gather(left_wide, 'blk', axis=0, tiled=True)  15.1 us
  transfers between devices with their start and end apart: 1, of which 1 were waited for; matrix products, arithmetic and copies ran while one was open for 0% of the time, Pallas kernels for 0%

profile of v1, /device:TPU:0, one launch (start us, length us, event | category | flops | bytes accessed | tf_op | source)
XLA Modules:
  0.0 473.4 jit_solution(7564404267348109461)
XLA Ops:
  7.9 15.1 %all_gather.15 = f32[512,64]{0,1:T(8,128)S(1)} all-gather(f32[128,64]{0,1:T(8,128)S(1)} %convert_element_type.55), channel_id=1, replica_groups=mesh['wide'=8,'blk'=4] {'blk'}, dimensions={0}, use_global_device_ids=true | all-gather | bytes 163840 | tf_op jit(solution)/shard_map/all_gather | solution.py:134
  23.7 11.2 %all-gather.1 = s32[4,1,128]{2,1,0:T(1,128)S(1)} all-gather(s32[1,1,128]{2,1,0:T(1,128)S(1)} %bitcast.84), channel_id=1, replica_groups=mesh['wide'=8,'blk'=4] {'blk'}, dimensions={0}, use_global_device_ids=true | all-gather | bytes 2560 | tf_op jit(solution)/shard_map/all_gather | solution.py:133
  35.6 7.7 %all-gather.2 = f32[4,1,128]{2,1,0:T(1,128)S(1)} all-gather(f32[1,1,128]{2,1,0:T(1,128)S(1)} %bitcast.85), channel_id=1, replica_groups=mesh['wide'=8,'blk'=4] {'blk'}, dimensions={0}, use_global_device_ids=true | all-gather | bytes 2560 | tf_op jit(solution)/shard_map/all_gather | solution.py:132
  45.3 1.1 fusion.28
  46.4 1.0 fusion.33
  48.2 19.8 %reduce-scatter.2.cloned.1.call-done = f32[128,128]{0,1:T(8,128)} async-done(((f32[512,128]{0,1:T(8,128)}), f32[128,128]{0,1:T(8,128)}) %reduce-scatter.2.cloned.1.call-update) | async-done | bytes 65552 | tf_op jit(solution)/shard_map/reduce_scatter | solution.py:149
  67.9 1.0 fusion.55
  68.9 38.6 %psum.7 = f32[64,64]{1,0:T(8,128)S(1)} all-reduce(f32[64,64]{1,0:T(8,128)S(1)} %fusion.55), channel_id=1, replica_groups=mesh['wide'=8,'blk'=4] {'wide','blk'}, use_global_device_ids=true, to_apply=%region_1.2 | all-reduce | flops 4096 | bytes 32768 | tf_op jit(solution)/shard_map/psum | solution.py:156
  107.7 94.5 %while.57 = (s32[]{:T(128)}, f32[64,64]{1,0:T(8,128)S(1)}, f32[64,64]{0,1:T(8,128)S(1)}, s32[]{:T(128)}, s32[]{:T(128)}) while((s32[]{:T(128)}, f32[64,64]{1,0:T(8,128)S(1)}, f32[64,64]{0,1:T(8,128)S(1)}, s32[]{:T(128)}, s32[]{:T(128)}) %tuple.124), condition=%wide.region_3.4_spmd.clone.clone, body=%wide.region_2.3_spmd.clone.clone.sunk | while | flops 66051 | bytes 101992 | solution.py:27
  202.2 93.7 %while.55 = (s32[]{:T(128)}, f32[64,128]{1,0:T(8,128)S(1)}, f32[64,128]{1,0:T(8,128)S(1)}, f32[64,64]{1,0:T(8,128)S(1)}, s32[]{:T(128)}, /*index=5*/s32[]{:T(128)}, s32[]{:T(128)}) while((s32[]{:T(128)}, f32[64,128]{1,0:T(8,128)S(1)}, f32[64,128]{1,0:T(8,128)S(1)}, f32[64,64]{1,0:T(8,128)S(1)}, s32[]{:T(128)}, ...), condition=%wide.region_5.6_spmd.clone, body=%wide.region_4.5_spmd.clone.sunk | while | flops 131460 | bytes 102520 | solution.py:42
  202.8 0.8 fusion.76
  204.3 0.8 fusion.76
  205.8 0.8 fusion.76
  207.2 0.8 fusion.76
  208.7 0.8 fusion.76
  210.1 0.8 fusion.76
  211.6 0.8 fusion.76
  213.1 0.8 fusion.76
  214.5 0.8 fusion.76
  216.0 0.8 fusion.76
  217.5 0.8 fusion.76
  218.9 0.8 fusion.76
  220.4 0.8 fusion.76
  221.9 0.8 fusion.76
  223.3 0.8 fusion.76
  224.8 0.8 fusion.76
  226.2 0.8 fusion.76
  227.7 0.8 fusion.76
  229.2 0.8 fusion.76
  230.6 0.8 fusion.76
  232.1 0.8 fusion.76
  233.6 0.8 fusion.76
  235.0 0.8 fusion.76
  236.5 0.8 fusion.76
  238.0 0.8 fusion.76
  239.4 0.8 fusion.76
  240.9 0.8 fusion.76
  242.4 0.8 fusion.76
  243.8 0.8 fusion.76
  245.3 0.8 fusion.76
  246.7 0.8 fusion.76
  248.2 0.8 fusion.76
  249.7 0.8 fusion.76
  251.1 0.8 fusion.76
  252.6 0.8 fusion.76
  270.2 0.8 fusion.76
  273.1 0.8 fusion.76
  276.0 0.8 fusion.76
  279.0 0.8 fusion.76
  296.6 75.5 %all-gather = f32[2048,64]{1,0:T(8,128)S(1)} all-gather(f32[64,64]{1,0:T(8,128)S(1)} %fusion.53), channel_id=2, replica_groups=mesh['wide'=8,'blk'=4] {'wide','blk'}, dimensions={0}, use_global_device_ids=true | all-gather | bytes 540672 | tf_op jit(solution)/shard_map/all_gather | solution.py:160
  372.3 93.7 %while.56 = (s32[]{:T(128)}, f32[64,64]{1,0:T(8,128)S(1)}, f32[64,64]{1,0:T(8,128)S(1)}, f32[64,64]{1,0:T(8,128)S(1)}, s32[]{:T(128)}, /*index=5*/s32[]{:T(128)}, s32[]{:T(128)}, s32[]{:T(128)}) while((s32[]{:T(128)}, f32[64,64]{1,0:T(8,128)S(1)}, f32[64,64]{1,0:T(8,128)S(1)}, f32[64,64]{1,0:T(8,128)S(1)}, s32[]{:T(128)}, ...), condition=%wide.region_8.9_spmd.clone, body=%wide.region_7.8_spmd.clone.sunk | while | flops 65800 | bytes 69297 | solution.py:58
  375.8 0.8 fusion.79
  383.1 0.8 fusion.79
  389.0 0.8 fusion.79
  396.3 0.8 fusion.79
  403.6 0.8 fusion.79
  410.9 0.8 fusion.79
  416.8 0.8 fusion.79
  424.1 0.8 fusion.79
  431.4 0.8 fusion.79
  438.7 0.8 fusion.79
  444.6 0.8 fusion.79
  451.9 0.8 fusion.79
  459.2 0.8 fusion.79
  (881 shorter events, 207.1 us)
Async XLA Ops:
  7.2 37.4 %copy-start = (bf16[512,64]{0,1:T(8,128)(2,1)S(1)}, bf16[512,64]{0,1:T(8,128)(2,1)}, u32[]{:S(2)}) copy-start(bf16[512,64]{0,1:T(8,128)(2,1)} %param.19) | copy-start | bytes 196612
  7.2 60.7 %reduce-scatter.2.cloned.1.call-start = ((), (), s32[]{:S(2)}) async-start(), calls=%async_computation.1 | async-start | bytes 327680 | tf_op jit(solution)/shard_map/reduce_scatter | solution.py:149
  23.0 0.7 copy-start.6
  34.9 0.7 copy-start.7
  35.6 7.7 %copy-start.5 = (bf16[512]{0:T(512)(128)(2,1)S(1)}, bf16[512]{0:T(512)(128)(2,1)}, u32[]{:S(2)}) copy-start(bf16[512]{0:T(512)(128)(2,1)} %param.21) | copy-start | bytes 3076
  43.3 0.7 copy-start.4
  44.6 0.7 copy-start.8
  44.6 0.7 copy-start.9
  107.7 94.5 %copy-start.3 = (f32[128,128]{0,1:T(8,128)S(1)}, f32[128,128]{0,1:T(8,128)}, u32[]{:S(2)}) copy-start(f32[128,128]{0,1:T(8,128)} %reduce-scatter.2.cloned.1.call-done) | copy-start | bytes 196612
  295.9 0.6 copy-start.1
  466.0 0.6 copy-start.2
Sparse Core Ops, SparseCore 0:
  48.2 19.6 reduce-scatter.1
